TPU v7x, 512 devices: a whole 4x8x8 slice. The times are simulated.
512 devices in a mesh: sub: 16 (over x_lo, y), elem: 32 (over z, x_hi, core).
Axes of the slice: x: 4 (x_hi: 2, x_lo: 2; x = x_hi * 2 + x_lo), y: 8, z: 8, core: 2. Of those that a mesh axis runs over, the one named last changes fastest.
Arguments:
- element_tiles: bfloat16 [4096, 128, 128], P(('sub', 'elem')), parts along dimension 0, may hold values from -0.5 to 0.5
- element_blocks: int32 [4096, 2], P(('sub', 'elem')), parts along dimension 0, may hold values from 0 to 31
- mode_shapes: bfloat16 [65536, 1024], P(('sub', 'elem')), parts along dimension 0, may hold values from -0.5 to 0.5
- trial_modes: bfloat16 [16384, 128], P('sub'), parts along dimension 0, may hold values from -0.1875 to 0.1875
Outputs:
- reduced_stiffness: float32 [16384, 1024], P(('sub', 'elem')), parts along dimension 0
- interface_forces: float32 [16384, 128], P(('sub', 'elem')), parts along dimension 0
There are 16 independent parts, one for each index of `sub`. A program takes and returns all parts, laid end to end along the dimension named above; each array names one. Nothing has to cross between parts.
Inputs may be any that keep to these rules, and one draw needn't show every extreme that they name: `element_blocks`: each row gives the row block and the column block of one element tile.
All inputs are finite; a program needn't handle non-finite values.
Results may differ from a plain program's by a relative error of at most 0.0029.
Values may be sent and summed in bfloat16 or wider, within the bound.
A program may use at most 64 MiB of HBM per device.

v0:
```python
import jax
import jax.numpy as jnp
from jax import lax
from jax.sharding import Mesh
from jax.sharding import PartitionSpec as P

ELEM = ("elem_0", "elem_1", "elem_2")
SUB_ELEM = ("sub", "elem_0", "elem_1", "elem_2")


def in_blocks(array, dim, length):
    lengths = array.shape
    parts = array.reshape(*lengths[:dim], length, lengths[dim] // length, *lengths[dim + 1 :])
    return jnp.moveaxis(parts, dim, 0)


def sent_and_summed(array, axis, dim):
    parts = in_blocks(array, dim, lax.axis_size(axis))
    arrived = lax.all_to_all(parts, axis, split_axis=0, concat_axis=0, tiled=True)
    return arrived.sum(axis=0)


def summed_rows(array, axes, dim):
    far, near = axes
    parts = in_blocks(array, dim, lax.axis_size(far))
    nearer = sent_and_summed(parts, near, dim + 1)
    arrived = lax.all_to_all(nearer, far, split_axis=0, concat_axis=0, tiled=True)
    return arrived.sum(axis=0)


def project(row_side, stiff_modes):
    return lax.dot_general(
        row_side, stiff_modes, (((0,), (0,)), ((), ())), preferred_element_type=jnp.float32
    )


def body(element_tiles, element_blocks, mode_shapes, trial_modes):
    gathered = lax.all_gather(mode_shapes, ELEM, axis=0, tiled=True)
    block_width = element_tiles.shape[1]
    mode_count = gathered.shape[1]
    blocks = gathered.reshape(-1, block_width, mode_count)
    row_side = jnp.take(blocks, element_blocks[:, 0], axis=0).reshape(-1, mode_count)
    col_side = jnp.take(blocks, element_blocks[:, 1], axis=0)
    stiff_modes = jnp.einsum(
        "eij,ejm->eim", element_tiles, col_side, preferred_element_type=jnp.float32
    )
    stiff_modes = stiff_modes.astype(jnp.bfloat16).reshape(-1, mode_count)
    reduced = summed_rows(project(row_side, stiff_modes), (("elem_0", "elem_1"), "elem_2"), 0)
    forces = jnp.dot(reduced, trial_modes.astype(jnp.float32), precision=lax.Precision.HIGHEST)
    return (reduced, forces)


def solution(mesh):
    split = Mesh(
        mesh.devices.reshape(mesh.shape["sub"], 8, 2, 2), ("sub", "elem_0", "elem_1", "elem_2")
    )
    placed = (P(SUB_ELEM, None, None), P(SUB_ELEM, None), P(SUB_ELEM, None), P("sub", None))
    return jax.shard_map(
        body,
        mesh=split,
        in_specs=placed,
        out_specs=(P(SUB_ELEM, None), P(SUB_ELEM, None)),
        check_vma=False,
    )
```

profile of v0, /device:TPU:1, one launch (start us, length us, event | category | flops | bytes accessed | tf_op | source)
XLA Modules:
  0.0 218.3 jit_solution(14570754254697076420)
XLA Ops:
  7.2 0.0 copy-start
  7.2 0.0 all-gather.2.cloned.1.call-start
  7.2 0.7 all-gather.2.cloned.1.call-update
  7.9 0.8 compare_and_fusion
  8.7 116.1 %all-gather.2.cloned.1.call-done = bf16[4096,1024]{1,0:T(8,128)(2,1)} async-done(((bf16[128,1024]{1,0:T(8,128)(2,1)}), bf16[4096,1024]{1,0:T(8,128)(2,1)}) %all-gather.2.cloned.1.call-update) | async-done | bytes 8388624 | tf_op jit(solution)/shard_map/all_gather | solution.py:38
  124.8 4.1 %gather_fusion = bf16[8,128,1024]{2,1,0:T(8,128)(2,1)S(1)} fusion(bf16[32,128,1024]{2,1,0:T(8,128)(2,1)} %bitcast.26, s32[1024]{0:T(1024)S(1)} %get-tuple-element.10), kind=kCustom, calls=%fused_computation.clone | custom fusion | bytes 4194336 | tf_op jit(solution)/shard_map/jit(_take)/gather | solution.py:42
  128.8 1.6 broadcast_select_fusion
  130.4 3.9 %copy.9 = bf16[1024,1024]{0,1:T(8,128)(2,1)} copy(bf16[1024,1024]{1,0:T(8,128)(2,1)} %bitcast.25) | data formatting | bytes 4194304 | tf_op jit(solution)/shard_map/reshape | solution.py:42
  134.3 4.1 %gather_fusion.1 = bf16[8,128,1024]{2,1,0:T(8,128)(2,1)S(1)} fusion(bf16[32,128,1024]{2,1,0:T(8,128)(2,1)} %bitcast.27, s32[1024]{0:T(1024)S(1)} %get-tuple-element.9), kind=kCustom, calls=%fused_computation.1.clone | custom fusion | bytes 4194336 | tf_op jit(solution)/shard_map/jit(_take)/gather | solution.py:43
  138.4 0.0 copy-done
  138.4 0.0 copy-start.1
  138.4 0.8 fusion.3
  139.2 0.8 copy-done.1
  140.0 2.3 %convolution_bitcast_fusion = f32[2,16,32,1024]{3,2,0,1:T(8,128)S(1)} fusion(bf16[16,2,32,1024]{3,2,1,0:T(8,128)(2,1)S(1)} %bitcast.28, bf16[1024,1024,1,1]{1,0,3,2:T(8,128)(2,1)S(1)} %bitcast.29), kind=kOutput, calls=%fused_computation.2 | convolution fusion | flops 2147483648 | bytes 8388608 | tf_op jit(solution)/shard_map/dot_general | solution.py:32
  142.3 0.6 copy.10
  142.9 8.0 %all_to_all.10 = f32[2,16,32,1024]{3,2,1,0:T(8,128)} all-to-all(f32[2,16,32,1024]{3,2,1,0:T(8,128)S(1)} %copy.10), channel_id=1, replica_groups=mesh['sub'=16,'elem_0'=8,'elem_1'=2,'elem_2'=2] {'elem_2'}, dimensions={0} | all-to-all | bytes 8388608 | tf_op jit(solution)/shard_map/all_to_all | solution.py:19
  151.0 2.8 %reduce_sum.18 = f32[16,32,1024]{2,1,0:T(8,128)S(1)} reduce(f32[2,16,32,1024]{3,2,1,0:T(8,128)} %all_to_all.10, f32[]{:T(128)} %constant.1.clone.1), dimensions={0}, to_apply=%region_0.0 | reduce | flops 524288 | bytes 6291460 | tf_op jit(solution)/shard_map/reduce_sum | solution.py:20
  153.8 55.1 %all_to_all.11 = f32[16,32,1024]{2,1,0:T(8,128)} all-to-all(f32[16,32,1024]{2,1,0:T(8,128)S(1)} %reduce_sum.18), channel_id=1, replica_groups=mesh['sub'=16,'elem_0'=8,'elem_1'=2,'elem_2'=2] {'elem_0','elem_1'}, dimensions={0} | all-to-all | bytes 4194304 | tf_op jit(solution)/shard_map/all_to_all | solution.py:27
  208.8 0.0 copy-start.3
  208.8 1.8 reduce_sum.19
  210.6 0.0 copy-done.3
  210.6 0.0 copy-start.2
  210.6 0.8 fusion.8
  211.5 0.0 copy-done.2
  (1 shorter events, 0.0 us)
Async XLA Ops:
  7.2 131.3 %copy-start = (bf16[8,128,128]{2,1,0:T(8,128)(2,1)S(1)}, bf16[8,128,128]{2,1,0:T(8,128)(2,1)}, u32[]{:S(2)}) copy-start(bf16[8,128,128]{2,1,0:T(8,128)(2,1)} %param.6) | copy-start | bytes 786436
  7.2 117.6 %all-gather.2.cloned.1.call-start = ((), (), s32[]{:S(2)}) async-start(), calls=%async_computation.2 | async-start | bytes 8650752 | tf_op jit(solution)/shard_map/all_gather | solution.py:38
  138.4 1.6 copy-start.1
  208.8 1.8 copy-start.3
  210.6 0.9 copy-start.2
Sparse Core Ops, SparseCore 0:
  11.4 113.3 all-gather.1
where the time goes:
time: 220 us; the launch traced here: 218 us
  waiting for transfers between devices  117 us (53%)
  blocking collectives  63.1 us (29%)
  between operations  14.1 us (6%)
  local copies, waits for them, and re-layouts  13.4 us (6%)
  other arithmetic  6.89 us (3%)
  matrix products  3.95 us (2%)
    all_gather x1, waiting for transfers between devices, body(): gathered = lax.all_gather(mode_shapes, ELEM, axis=0, tiled=True)  116 us
    all_to_all x1, blocking collectives, summed_rows(): lax.all_to_all(nearer, far, split_axis=0, concat_axis=0, tiled=True)  55.1 us
    all_to_all x1, blocking collectives, sent_and_summed(): lax.all_to_all(parts, axis, split_axis=0, concat_axis=0, tiled=True)  8.04 us
  transfers between devices with their start and end apart: 1, of which 1 were waited for; matrix products, arithmetic and copies ran while one was open for 0% of the time, Pallas kernels for 0%

commit v1 on v0

v1 whole, which is shorter than its diff:
```python
import functools

import jax
import jax.numpy as jnp
from jax import lax
from jax.experimental import pallas as pl
from jax.experimental.pallas import tpu as pltpu
from jax.sharding import PartitionSpec as P

MESH = pl.DeviceIdType.MESH
NZ = 8
PIECES = 2


def kernel(tiles, blocks, modes, trial, reduced, forces, pbuf, turned, tbuf, ids, stiff, out_parts, in_parts, tr,
           own_sem, p_send, p_recv, s_recv, t_send, t_recv, i_send, i_recv, r_send, r_recv):
    e = lax.axis_index("elem")
    c = lax.rem(e, 2)
    xh = lax.rem(e // 2, 2)
    z = e // 4
    q = lax.rem(e, 4)
    s = 1 - 2 * c
    rows = modes.shape[0] // PIECES
    per = tiles.shape[0]
    wide = stiff.shape[0]

    def rank(dz, other_x=False, other_c=False):
        level = lax.rem(z + dz + 2 * NZ, NZ)
        return level * 4 + 2 * (1 - xh if other_x else xh) + (1 - c if other_c else c)

    ahead, behind, across, beside = rank(s), rank(-s), rank(0, True), rank(0, False, True)
    barrier = pltpu.get_barrier_semaphore()
    for device in (ahead, behind, across, beside):
        pl.semaphore_signal(barrier, inc=1, device_id={"elem": device}, device_id_type=MESH)
    pl.semaphore_wait(barrier, 4)

    waits = []

    def put(src, dst, send, recv, device):
        copy = pltpu.make_async_remote_copy(
            src_ref=src, dst_ref=dst, send_sem=send, recv_sem=recv, device_id={"elem": device}, device_id_type=MESH
        )
        copy.start()
        waits.append(copy)

    counter = [0]

    def send_piece(src, block, p, slot, device, beside_slot=None):
        n = counter[0]
        counter[0] += 1
        dst = pbuf.at[block, pl.ds(p * rows, rows)]
        recv = p_recv.at[slot, p] if beside_slot is None else s_recv.at[beside_slot, p]
        put(src, dst, p_send.at[n], recv, device)

    block_of = {}
    for j in range(1, 5):
        block_of[j - 1] = rank(-j * s)
    for j in range(1, 4):
        block_of[3 + j] = rank(j * s)
    for j in range(0, 5):
        block_of[7 + j] = rank(-j * s, True)
    for j in range(1, 4):
        block_of[11 + j] = rank(j * s, True)
    block_of[15] = e

    def arrived(slot, p):
        part = pbuf.at[block_of[slot], pl.ds(p * rows, rows)]
        pltpu.make_async_remote_copy(
            src_ref=part, dst_ref=part, send_sem=p_send.at[0], recv_sem=p_recv.at[slot, p],
            device_id={"elem": e}, device_id_type=MESH,
        ).wait_recv()
        return part

    keep = pltpu.make_async_copy(modes, pbuf.at[e], own_sem.at[0])
    keep.start()
    for p in range(PIECES):
        part = modes.at[pl.ds(p * rows, rows)]
        send_piece(part, e, p, 0, ahead)
        send_piece(part, e, p, 7, across)
        send_piece(part, e, p, 4, behind)
    for p in range(PIECES):
        send_piece(modes.at[pl.ds(p * rows, rows)], e, p, None, beside, 15)
    put(blocks, ids.at[1], i_send.at[0], i_recv.at[0], beside)
    put(blocks, ids.at[2], i_send.at[1], i_recv.at[1], across)
    put(tiles, tbuf.at[1], t_send.at[0], t_recv.at[0], beside)
    put(tiles, tbuf.at[2], t_send.at[1], t_recv.at[1], across)
    keep_t = pltpu.make_async_copy(tiles, tbuf.at[0], own_sem.at[1])
    keep_t.start()
    keep_i = pltpu.make_async_copy(blocks, ids.at[0], own_sem.at[2])
    keep_i.start()
    keep_r = pltpu.make_async_copy(trial, tr, own_sem.at[3])
    keep_r.start()

    for r in range(5):
        for p in range(PIECES):
            if r + 1 <= 4:
                part = arrived(r, p)
                if r + 1 < 4:
                    send_piece(part, block_of[r], p, r + 1, ahead)
                send_piece(part, block_of[r], p, None, beside, r)
            part = arrived(7 + r, p)
            if r < 4:
                send_piece(part, block_of[7 + r], p, 8 + r, ahead)
            send_piece(part, block_of[7 + r], p, None, beside, 7 + r)
            if r + 1 <= 3:
                part = arrived(4 + r, p)
                if r + 1 < 3:
                    send_piece(part, block_of[4 + r], p, 5 + r, behind)
                send_piece(part, block_of[4 + r], p, 12 + r, across)
                send_piece(part, block_of[4 + r], p, None, beside, 4 + r)
            if 1 <= r <= 3:
                part = arrived(11 + r, p)
                send_piece(part, block_of[11 + r], p, None, beside, 11 + r)
        if r == 1:
            pltpu.make_async_copy(tbuf.at[2], tbuf.at[2], t_recv.at[1]).wait()
            put(tbuf.at[2], tbuf.at[3], t_send.at[2], t_recv.at[2], beside)
            pltpu.make_async_copy(ids.at[2], ids.at[2], i_recv.at[1]).wait()
            put(ids.at[2], ids.at[3], i_send.at[2], i_recv.at[2], beside)
    for slot in range(16):
        block = block_of[slot]
        other = lax.rem(block, 2)
        level = block // 4
        mirrored = lax.rem(2 * z - level + 2 * NZ, NZ)
        theirs = mirrored * 4 + 2 * lax.rem(block // 2, 2) + 1 - other
        for p in range(PIECES):
            part = pbuf.at[theirs, pl.ds(p * rows, rows)]
            pltpu.make_async_copy(part, part, s_recv.at[slot, p]).wait()
    keep.wait()
    keep_t.wait()
    keep_i.wait()
    for k, (sem_t, sem_i) in enumerate(((0, 0), (2, 2))):
        slot = 1 + 2 * k
        pltpu.make_async_copy(tbuf.at[slot], tbuf.at[slot], t_recv.at[sem_t]).wait()
        pltpu.make_async_copy(ids.at[slot], ids.at[slot], i_recv.at[sem_i]).wait()

    cols = pl.ds(pl.multiple_of(q * wide, wide), wide)

    @pl.loop(0, NZ * 4)
    def _(b):
        turned[b] = pbuf[b, :, cols].T

    for g in range(4):
        for i in range(per):
            lhs = turned[ids[g, i, 1]]
            got = lax.dot_general(lhs, tbuf[g, i], (((1,), (1,)), ((), ())), preferred_element_type=jnp.float32)
            k = g * per + i
            stiff[:, k * 128 : (k + 1) * 128] = got.astype(jnp.bfloat16)

    def parts_for(m):
        span = pl.ds(pl.multiple_of(m * 256, 256), 256)
        acc = jnp.zeros((wide, 256), jnp.float32)
        for k in range(0, 4 * per, 2):
            first = pbuf[ids[k // per, k % per, 0], :, span]
            second = pbuf[ids[(k + 1) // per, (k + 1) % per, 0], :, span]
            acc += jnp.dot(
                stiff[:, k * 128 : (k + 2) * 128], jnp.concatenate([first, second], axis=0),
                preferred_element_type=jnp.float32,
            )
        out_parts[span, :] = acc.T.astype(jnp.bfloat16)

    order = (2, 1, 3, 0)
    for n, dm in enumerate(order):
        m = lax.rem(z // 2 + dm, 4)
        parts_for(m)
        for w in range(8):
            if dm == 0:
                target = lax.rem(z, 2) * 4 + q + 1 + w
                target = m * 8 + lax.rem(target, 8)
                if w == 7:
                    in_parts[e] = out_parts[pl.ds(pl.multiple_of(e * 32, 32), 32), :]
                    continue
            else:
                target = m * 8 + w
            k = n * 8 + w
            put(
                out_parts.at[pl.ds(pl.multiple_of(target * 32, 32), 32)], in_parts.at[e],
                r_send.at[k], r_recv.at[e], target,
            )
    for k in range(1, 32):
        source = lax.rem(e + k, 32)
        pltpu.make_async_copy(in_parts.at[source], in_parts.at[source], r_recv.at[source]).wait()
    for quarter in range(4):
        total = jnp.zeros((32, wide), jnp.float32)
        for level in range(NZ):
            total += in_parts[level * 4 + quarter].astype(jnp.float32)
        reduced[:, quarter * wide : (quarter + 1) * wide] = total
    keep_r.wait()
    forces[...] = jnp.dot(
        reduced[...], tr[...].astype(jnp.float32), precision=lax.Precision.HIGHEST, preferred_element_type=jnp.float32
    )
    for copy in waits:
        copy.wait_send()


def body(element_tiles, element_blocks, mode_shapes, trial_modes):
    block, count = mode_shapes.shape
    per = element_tiles.shape[0]
    wide = count // 4
    anywhere = pl.BlockSpec(memory_space=pl.ANY)
    in_vmem = pl.BlockSpec(memory_space=pltpu.VMEM)
    dma = pltpu.SemaphoreType.DMA
    return pl.pallas_call(
        kernel,
        out_shape=(
            jax.ShapeDtypeStruct((count // 32, count), jnp.float32),
            jax.ShapeDtypeStruct((count // 32, trial_modes.shape[1]), jnp.float32),
        ),
        in_specs=[anywhere, pl.BlockSpec(memory_space=pltpu.SMEM), anywhere, anywhere],
        out_specs=(in_vmem, in_vmem),
        scratch_shapes=[
            pltpu.VMEM((NZ * 4, block, count), jnp.bfloat16),
            pltpu.VMEM((NZ * 4, wide, block), jnp.bfloat16),
            pltpu.VMEM((4, per, block, block), jnp.bfloat16),
            pltpu.SMEM((4, per, 2), jnp.int32),
            pltpu.VMEM((wide, 4 * per * block), jnp.bfloat16),
            pltpu.VMEM((count, wide), jnp.bfloat16),
            pltpu.VMEM((NZ * 4, count // 32, wide), jnp.bfloat16),
            pltpu.VMEM(trial_modes.shape, jnp.bfloat16),
            dma((4,)),
            dma((31 * PIECES,)),
            dma((15, PIECES)),
            dma((16, PIECES)),
            dma((3,)),
            dma((3,)),
            dma((3,)),
            dma((3,)),
            dma((31 + 1,)),
            dma((32,)),
        ],
        compiler_params=pltpu.CompilerParams(collective_id=0, has_side_effects=True),
        name="project",
    )(element_tiles, element_blocks, mode_shapes, trial_modes)


def solution(mesh):
    every = P(("sub", "elem"), None)
    return jax.shard_map(
        body,
        mesh=mesh,
        in_specs=(P(("sub", "elem"), None, None), every, every, P("sub", None)),
        out_specs=(every, every),
        check_vma=False,
    )
```

time: 220 us -> 72.8 us (0.33)
  waiting for transfers between devices: 117 us -> 0 us
  Pallas kernels: 0 us -> 68.5 us
  blocking collectives: 63.1 us -> 0 us
  between operations: 14.1 us -> 0.65 us
  local copies, waits for them, and re-layouts: 13.4 us -> 3.53 us
  other arithmetic: 6.89 us -> 0 us
  matrix products: 3.95 us -> 0 us
    all_gather x1 -> x0, waiting for transfers between devices: 116 us -> none  [body(): gathered = lax.all_gather(mode_shapes, ELEM, axis=0, tiled=True)]
    pallas_call x0 -> x1, Pallas kernels: none -> 68.5 us  [body(): pl.pallas_call(kernel, out_shape=(jax.ShapeDtypeStruct((count // 32, coun...]
    all_to_all x2 -> x0, blocking collectives: 63.1 us -> none  [the longest x1 55.1 us: summed_rows(): lax.all_to_all(nearer, far, split_axis=0, concat_axis=0, tiled=True)]
    gather x2 -> x0, local copies, waits for them, and re-layouts: 8.12 us -> none  [the longest x1 4.06 us: body(): jnp.take(blocks, element_blocks[:, 0], axis=0).reshape(-1, mode_count)]
    reduce_sum x2 -> x0, other arithmetic: 4.55 us -> none  [the longest x1 2.79 us: sent_and_summed(): return arrived.sum(axis=0)]
    dot_general x3 -> x0, matrix products: 3.95 us -> none  [the longest x1 2.33 us: project(): lax.dot_general(row_side, stiff_modes, (((0,), (0,)), ((), ())), preferre...]
    reshape x1 -> x0, local copies, waits for them, and re-layouts: 3.92 us -> none  [body(): jnp.take(blocks, element_blocks[:, 0], axis=0).reshape(-1, mode_count)]
    unnamed x8 -> x5, local copies, waits for them, and re-layouts: 0.82 us -> 3.53 us
  transfers between devices with their start and end apart: 1 -> 0, of which waited for: 1 -> 0; matrix products, arithmetic and copies ran while one was open for 0% -> 0% of each run, Pallas kernels for 0% -> 0%
where the time goes in v1:
time: 72.8 us; the launch traced here: 72.6 us
  Pallas kernels  68.5 us (94%)
  local copies, waits for them, and re-layouts  3.53 us (5%)
    pallas_call x1, Pallas kernels, body(): pl.pallas_call(kernel, out_shape=(jax.ShapeDtypeStruct((count // 32, coun...  68.5 us
    unnamed x5, local copies, waits for them, and re-layouts  3.53 us

profile of v1, /device:TPU:1, one launch (start us, length us, event | category | flops | bytes accessed | tf_op | source)
XLA Modules:
  0.0 72.6 jit_solution(18212622457114038192)
XLA Ops:
  0.6 1.3 %copy.6.blocks = s32[8,2]{1,0:T(8,128)} copy(s32[8,2]{0,1:T(2,128)} %param.5) | data formatting | bytes 128 | tf_op args[1]
  2.0 68.5 %project.1 = (f32[32,1024]{1,0:T(8,128)}, f32[32,128]{1,0:T(8,128)}) custom-call(bf16[8,128,128]{2,1,0:T(8,128)(2,1)} %tiles.1, s32[8,2]{1,0:T(8,128)} %copy.6.blocks, bf16[128,1024]{1,0:T(8,128)(2,1)} %modes.1, bf16[1024,128]{1,0:T(8,128)(2,1)} %trial.1), custom_call_target="tpu_custom_call" | custom-call | tf_op jit(solution)/shard_map/project/pallas_call | solution.py:202
  70.4 0.0 copy-start
  70.5 1.6 %copy.9 = f32[32,1024]{1,0:T(8,128)} copy(f32[32,1024]{1,0:T(8,128)} %get-tuple-element.4) | data formatting | bytes 262144
  72.0 0.0 copy-done
  72.0 0.6 copy.10
Async XLA Ops:
  70.4 1.6 %copy-start = (f32[32,128]{1,0:T(8,128)S(1)}, f32[32,128]{1,0:T(8,128)}, u32[]{:S(2)}) copy-start(f32[32,128]{1,0:T(8,128)} %get-tuple-element.5) | copy-start | bytes 49156

commit v2 on v0

v2 whole, which is shorter than its diff:
```python
import jax
import jax.numpy as jnp
from jax import lax
from jax.experimental import pallas as pl
from jax.experimental.pallas import tpu as pltpu
from jax.sharding import PartitionSpec as P

MESH = pl.DeviceIdType.MESH
NZ = 8
PIECES = 2
DEPTH = 4
CROSS = ((1, 0),)
SENDS = 31 * PIECES


def kernel(tiles, blocks, modes, trial, reduced, forces, pbuf, turned, tbuf, ids, stiff, part, going, coming, last, in_parts, tr,
           own_sem, p_send, p_recv, s_recv, t_send, t_recv, i_send, i_recv, g_send, g_recv, l_send, r_send, r_recv):
    e = lax.axis_index("elem")
    c = lax.rem(e, 2)
    xh = lax.rem(e // 2, 2)
    z = e // 4
    q = lax.rem(e, 4)
    rows = modes.shape[0] // PIECES
    per = tiles.shape[0]
    wide = stiff.shape[1]
    half = last.shape[1] // 2
    sign = [(1 - 2 * c) * (1 - 2 * (p % 2)) for p in range(PIECES)]

    def level(dz):
        return lax.rem(z + dz + 2 * NZ, NZ)

    def rank(dz, other_x=False, other_c=False):
        return level(dz) * 4 + 2 * (1 - xh if other_x else xh) + (1 - c if other_c else c)

    keep_i = pltpu.make_async_copy(blocks, ids.at[0], own_sem.at[2])
    keep_i.start()
    across, beside = rank(0, True), rank(0, False, True)
    barrier = pltpu.get_barrier_semaphore()
    for device in (rank(1), rank(-1), across, beside):
        pl.semaphore_signal(barrier, inc=1, device_id={"elem": device}, device_id_type=MESH)
    pl.semaphore_wait(barrier, 4)

    waits = []

    def put(src, dst, send, recv, device):
        copy = pltpu.make_async_remote_copy(
            src_ref=src, dst_ref=dst, send_sem=send, recv_sem=recv, device_id={"elem": device}, device_id_type=MESH
        )
        copy.start()
        waits.append(copy)

    def landed(ref, sem):
        pltpu.make_async_copy(ref, ref, sem).wait()

    first = {"A": -1, "B": 3, "C": 7, "D": 11}

    def block_of(kind, j, p, mine=True):
        turn = sign[p] if mine else -sign[p]
        dz = -j * turn if kind in "AC" else j * turn
        return rank(dz, kind in "CD", not mine)

    def piece_of(block, p):
        return pbuf.at[block, pl.ds(p * rows, rows)]

    counter = [0]

    def send_piece(src, block, p, device, recv):
        put(src, piece_of(block, p), p_send.at[counter[0]], recv, device)
        counter[0] += 1

    def forward(kind, j, p):
        block = block_of(kind, j, p)
        slot = first[kind] + j
        src = piece_of(block, p)
        landed(src, p_recv.at[slot, p])
        if (kind == "A" and j < 4) or (kind == "C" and j < 4 and (j + 1, p) not in CROSS):
            send_piece(src, block, p, rank(sign[p]), p_recv.at[slot + 1, p])
        if kind == "A" and (j, p) in CROSS:
            send_piece(src, block, p, across, p_recv.at[first["C"] + j, p])
        if kind == "B":
            if j < 3:
                send_piece(src, block, p, rank(-sign[p]), p_recv.at[slot + 1, p])
            send_piece(src, block, p, across, p_recv.at[first["D"] + j, p])
        send_piece(src, block, p, beside, s_recv.at[slot, p])

    backlog = []

    def turn_over(count):
        for _ in range(min(count, len(backlog))):
            block = backlog.pop(0)
            turned[block] = pbuf[block].T

    cols = pl.ds(pl.multiple_of(q * wide, wide), wide)
    keep = pltpu.make_async_copy(modes, pbuf.at[e], own_sem.at[0])
    keep.start()
    for p in range(PIECES):
        src = modes.at[pl.ds(p * rows, rows)]
        send_piece(src, e, p, rank(sign[p]), p_recv.at[first["A"] + 1, p])
        send_piece(src, e, p, across, p_recv.at[first["C"], p])
    for p in range(PIECES):
        src = modes.at[pl.ds(p * rows, rows)]
        send_piece(src, e, p, rank(-sign[p]), p_recv.at[first["B"] + 1, p])
    for p in range(PIECES):
        send_piece(modes.at[pl.ds(p * rows, rows)], e, p, beside, s_recv.at[15, p])
    keep_i.wait()
    put(ids.at[0], ids.at[1], i_send.at[0], i_recv.at[0], beside)
    put(tiles, tbuf.at[1], t_send.at[0], t_recv.at[0], beside)
    keep_t = pltpu.make_async_copy(tiles, tbuf.at[0], own_sem.at[1])
    keep_t.start()
    keep_r = pltpu.make_async_copy(trial, tr, own_sem.at[3])
    keep_r.start()

    def in_round(r):
        kinds = []
        if r < 4:
            kinds.append(("A", r + 1))
        if r < 3:
            kinds.append(("B", r + 1))
        kinds.append(("C", r))
        if 1 <= r <= 3:
            kinds.append(("D", r))
        return kinds

    def done_in(r, mine):
        if r < 3:
            near = [r + 1, -(r + 1)]
        else:
            near = [4] if r == 3 else []
        far = {0: [0], 4: [4]}.get(r, [r, -r])
        return [rank(d, False, not mine) for d in near] + [rank(d, True, not mine) for d in far]

    def from_beside(r):
        for kind, j in in_round(r):
            for p in range(PIECES):
                landed(piece_of(block_of(kind, j, p, False), p), s_recv.at[first[kind] + j, p])
        backlog.extend(done_in(r, False))

    for r in range(5):
        for kind, j in in_round(r):
            for p in range(PIECES):
                forward(kind, j, p)
                turn_over(3 if r == 4 else 2)
        if r == 1:
            put(tiles, tbuf.at[2], t_send.at[1], t_recv.at[1], across)
            put(ids.at[0], ids.at[2], i_send.at[1], i_recv.at[1], across)
        if r == 3:
            landed(tbuf.at[2], t_recv.at[1])
            put(tbuf.at[2], tbuf.at[3], t_send.at[2], t_recv.at[2], beside)
            landed(ids.at[2], i_recv.at[1])
            put(ids.at[2], ids.at[3], i_send.at[2], i_recv.at[2], beside)
        backlog.extend(done_in(r, True))
        if r == 0:
            keep.wait()
            backlog.append(e)
            for p in range(PIECES):
                landed(piece_of(rank(0, False, True), p), s_recv.at[15, p])
            backlog.append(beside)
            keep_t.wait()
        else:
            from_beside(r - 1)
    landed(tbuf.at[1], t_recv.at[0])
    landed(ids.at[1], i_recv.at[0])
    landed(tbuf.at[3], t_recv.at[2])
    landed(ids.at[3], i_recv.at[2])
    from_beside(4)
    turn_over(len(backlog))

    for g in range(4):
        for i in range(per):
            got = jnp.dot(tbuf[g, i], pbuf[ids[g, 1, i], :, cols], preferred_element_type=jnp.float32)
            k = g * per + i
            stiff[k * 128 : (k + 1) * 128, :] = got.astype(jnp.bfloat16)

    def parts_for(*pairs):
        spans = [pl.ds(pl.multiple_of(m * 256, 256), 256) for m in pairs]
        accs = [jnp.zeros((256, wide), jnp.float32) for _ in pairs]
        for k in range(0, 4 * per, DEPTH):
            which = [ids[n // per, 0, n % per] for n in range(k, k + DEPTH)]
            for n, span in enumerate(spans):
                some = jnp.concatenate([turned[b, span, :] for b in which], axis=1)
                accs[n] += jnp.dot(some, stiff[k * 128 : (k + DEPTH) * 128, :], preferred_element_type=jnp.float32)
        for n, span in enumerate(spans):
            part[span, :] = accs[n]

    def mine(dz, h):
        return part[pl.ds(pl.multiple_of(level(dz) * 2 * half + h * half, half), half), :]

    def step_on(way, step, h, value):
        going[way, step, h] = value.astype(jnp.bfloat16)
        n = (way * 2 + step) * 2 + h
        put(going.at[way, step, h], coming.at[way, step, h], g_send.at[n], g_recv.at[n], rank(1 - 2 * way))

    def come(way, step, h):
        landed(coming.at[way, step, h], g_recv.at[(way * 2 + step) * 2 + h])
        return coming[way, step, h].astype(jnp.float32)

    def rows_at(dz):
        return part[pl.ds(pl.multiple_of(level(dz) * 2 * half, half), 2 * half), :].astype(jnp.bfloat16)

    opposite = lax.rem(z // 2 + 2, 4)
    aside = 2 * lax.rem(z, 2) - 1
    parts_for(opposite, lax.rem(opposite + aside + 4, 4))
    order = (1 - xh, xh)
    for h in order:
        for way in range(2):
            step_on(way, 0, h, mine(3 - 6 * way, h))
    last[3] = rows_at(4)
    for k in range(4):
        put(last.at[3, pl.ds(k * 32, 32)], in_parts.at[12 + q], l_send.at[3 + k], r_recv.at[12 + q], level(4) * 4 + k)
    parts_for(lax.rem(opposite - aside + 4, 4), z // 2)
    last[2] = rows_at(0)
    for k in range(1, 4):
        other = lax.rem(q + k, 4)
        put(last.at[2, pl.ds(pl.multiple_of(other * 32, 32), 32)], in_parts.at[8 + q], l_send.at[k - 1], r_recv.at[8 + q], z * 4 + other)
    in_parts[8 + q] = last[2, pl.ds(pl.multiple_of(q * 32, 32), 32), :]
    for h in order:
        for way in range(2):
            step_on(way, 1, h, come(way, 0, h) + mine(2 - 4 * way, h))
    for h in order:
        for way in range(2):
            dz = 1 - 2 * way
            last[way, pl.ds(pl.multiple_of(h * half, half), half), :] = (come(way, 1, h) + mine(dz, h)).astype(jnp.bfloat16)
            for k in range(2):
                other = 2 * h + k
                put(
                    last.at[way, pl.ds(pl.multiple_of(other * 32, 32), 32)], in_parts.at[way * 4 + q],
                    r_send.at[way * 4 + other], r_recv.at[way * 4 + q], level(dz) * 4 + other,
                )
    for k in range(1, 4):
        other = lax.rem(q + k, 4)
        landed(in_parts.at[8 + other], r_recv.at[8 + other])
    for n in range(4):
        landed(in_parts.at[12 + n], r_recv.at[12 + n])
    for n in range(8):
        landed(in_parts.at[n], r_recv.at[n])
    for quarter in range(4):
        total = in_parts[8 + quarter].astype(jnp.float32) + in_parts[12 + quarter].astype(jnp.float32)
        total += in_parts[quarter].astype(jnp.float32) + in_parts[4 + quarter].astype(jnp.float32)
        reduced[:, quarter * wide : (quarter + 1) * wide] = total
    keep_r.wait()
    high = reduced[...].astype(jnp.bfloat16)
    rest = reduced[...] - high.astype(jnp.float32)
    middle = rest.astype(jnp.bfloat16)
    low = (rest - middle.astype(jnp.float32)).astype(jnp.bfloat16)
    terms = jnp.dot(jnp.concatenate([high, middle, low], axis=0), tr[...], preferred_element_type=jnp.float32)
    own = reduced.shape[0]
    forces[...] = terms[:own] + (terms[own : 2 * own] + terms[2 * own :])
    for copy in waits:
        copy.wait_send()


def body(element_tiles, element_blocks, mode_shapes, trial_modes):
    block, count = mode_shapes.shape
    per = element_tiles.shape[0]
    wide = count // 4
    own = count // 32
    outside = pl.BlockSpec(memory_space=pltpu.HBM)
    in_vmem = pl.BlockSpec(memory_space=pltpu.VMEM)
    dma = pltpu.SemaphoreType.DMA
    narrow, full = jnp.bfloat16, jnp.float32
    return pl.pallas_call(
        kernel,
        out_shape=(
            jax.ShapeDtypeStruct((own, count), full),
            jax.ShapeDtypeStruct((own, trial_modes.shape[1]), full),
        ),
        in_specs=[outside] * 4,
        out_specs=(in_vmem, in_vmem),
        scratch_shapes=[
            pltpu.VMEM((NZ * 4, block, count), narrow),
            pltpu.VMEM((NZ * 4, count, block), narrow),
            pltpu.VMEM((4, per, block, block), narrow),
            pltpu.SMEM((4, 2, per), jnp.int32),
            pltpu.VMEM((4 * per * block, wide), narrow),
            pltpu.VMEM((count, wide), full),
            pltpu.VMEM((2, 2, 2, 2 * own, wide), narrow),
            pltpu.VMEM((2, 2, 2, 2 * own, wide), narrow),
            pltpu.VMEM((4, 4 * own, wide), narrow),
            pltpu.VMEM((16, own, wide), narrow),
            pltpu.VMEM(trial_modes.shape, narrow),
            dma((4,)),
            dma((SENDS,)),
            dma((15, PIECES)),
            dma((16, PIECES)),
            dma((3,)),
            dma((3,)),
            dma((3,)),
            dma((3,)),
            dma((8,)),
            dma((8,)),
            dma((7,)),
            dma((8,)),
            dma((16,)),
        ],
        compiler_params=pltpu.CompilerParams(collective_id=0, has_side_effects=True, vmem_limit_bytes=56360960),
        name="project",
    )(element_tiles, element_blocks.T, mode_shapes, trial_modes)


def solution(mesh):
    every = P(("sub", "elem"), None)
    return jax.shard_map(
        body,
        mesh=mesh,
        in_specs=(P(("sub", "elem"), None, None), every, every, P("sub", None)),
        out_specs=(every, every),
        check_vma=False,
    )
```

time: 220 us -> 65.4 us (0.30)
  waiting for transfers between devices: 117 us -> 0 us
  blocking collectives: 63.1 us -> 0 us
  Pallas kernels: 0 us -> 62.7 us
  between operations: 14.1 us -> 0.65 us
  local copies, waits for them, and re-layouts: 13.4 us -> 1.93 us
  other arithmetic: 6.89 us -> 0 us
  matrix products: 3.95 us -> 0 us
    all_gather x1 -> x0, waiting for transfers between devices: 116 us -> none  [body(): gathered = lax.all_gather(mode_shapes, ELEM, axis=0, tiled=True)]
    all_to_all x2 -> x0, blocking collectives: 63.1 us -> none  [the longest x1 55.1 us: summed_rows(): lax.all_to_all(nearer, far, split_axis=0, concat_axis=0, tiled=True)]
    pallas_call x0 -> x1, Pallas kernels: none -> 62.7 us  [body(): pl.pallas_call(kernel, out_shape=(jax.ShapeDtypeStruct((own, count), full...]
    gather x2 -> x0, local copies, waits for them, and re-layouts: 8.12 us -> none  [the longest x1 4.06 us: body(): jnp.take(blocks, element_blocks[:, 0], axis=0).reshape(-1, mode_count)]
    reduce_sum x2 -> x0, other arithmetic: 4.55 us -> none  [the longest x1 2.79 us: sent_and_summed(): return arrived.sum(axis=0)]
    dot_general x3 -> x0, matrix products: 3.95 us -> none  [the longest x1 2.33 us: project(): lax.dot_general(row_side, stiff_modes, (((0,), (0,)), ((), ())), preferre...]
    reshape x1 -> x0, local copies, waits for them, and re-layouts: 3.92 us -> none  [body(): jnp.take(blocks, element_blocks[:, 0], axis=0).reshape(-1, mode_count)]
  transfers between devices with their start and end apart: 1 -> 0, of which waited for: 1 -> 0; matrix products, arithmetic and copies ran while one was open for 0% -> 0% of each run, Pallas kernels for 0% -> 0%
where the time goes in v2:
time: 65.4 us; the launch traced here: 65.3 us
  Pallas kernels  62.7 us (96%)
  local copies, waits for them, and re-layouts  1.93 us (3%)
    pallas_call x1, Pallas kernels, body(): pl.pallas_call(kernel, out_shape=(jax.ShapeDtypeStruct((own, count), full...  62.7 us
    unnamed x4, local copies, waits for them, and re-layouts  1.93 us

profile of v2, /device:TPU:1, one launch (start us, length us, event | category | flops | bytes accessed | tf_op | source)
XLA Modules:
  0.0 65.3 jit_solution(2706939073194710894)
XLA Ops:
  0.6 0.0 copy-start
  0.6 0.7 %copy-done = s32[8,2]{0,1:T(2,128)S(1)} copy-done((s32[8,2]{0,1:T(2,128)S(1)}, s32[8,2]{0,1:T(2,128)}, u32[]{:S(2)}) %copy-start) | copy-done | bytes 88
  1.3 62.7 %project.1 = (f32[32,1024]{1,0:T(8,128)S(1)}, f32[32,128]{1,0:T(8,128)S(1)}) custom-call(bf16[8,128,128]{2,1,0:T(8,128)(2,1)} %tiles.1, s32[2,8]{1,0:T(2,128)S(1)} %bitcast.1, bf16[128,1024]{1,0:T(8,128)(2,1)} %modes.1, bf16[1024,128]{1,0:T(8,128)(2,1)} %trial.1), custom_call_target="tpu_custom_call" | custom-call | tf_op jit(solution)/shard_map/project/pallas_call | solution.py:261
  64.0 0.7 %copy.8 = f32[32,1024]{1,0:T(8,128)} copy(f32[32,1024]{1,0:T(8,128)S(1)} %get-tuple-element.4) | data formatting | bytes 262144
  64.7 0.6 copy.9
Async XLA Ops:
  0.6 0.7 %copy-start = (s32[8,2]{0,1:T(2,128)S(1)}, s32[8,2]{0,1:T(2,128)}, u32[]{:S(2)}) copy-start(s32[8,2]{0,1:T(2,128)} %param.5) | copy-start | bytes 196

commit v3 on v2

--- a/solution.py
+++ b/solution.py
@@ -163,13 +163,16 @@
     landed(tbuf.at[3], t_recv.at[2])
     landed(ids.at[3], i_recv.at[2])
     from_beside(4)
-    turn_over(len(backlog))
 
     for g in range(4):
         for i in range(per):
             got = jnp.dot(tbuf[g, i], pbuf[ids[g, 1, i], :, cols], preferred_element_type=jnp.float32)
             k = g * per + i
             stiff[k * 128 : (k + 1) * 128, :] = got.astype(jnp.bfloat16)
+            if i % 2:
+                turn_over(1)
+
+    turn_over(len(backlog))
 
     def parts_for(*pairs):
         spans = [pl.ds(pl.multiple_of(m * 256, 256), 256) for m in pairs]

time: 65.4 us -> 65.4 us (level)
  no operation moved by 1% of the time
where the time goes in v3:
time: 65.4 us; the launch traced here: 65.3 us
  Pallas kernels  62.7 us (96%)
  local copies, waits for them, and re-layouts  1.93 us (3%)
    pallas_call x1, Pallas kernels, body(): pl.pallas_call(kernel, out_shape=(jax.ShapeDtypeStruct((own, count), full...  62.7 us
    unnamed x4, local copies, waits for them, and re-layouts  1.93 us

profile of v3, /device:TPU:1, one launch (start us, length us, event | category | flops | bytes accessed | tf_op | source)
XLA Modules:
  0.0 65.3 jit_solution(9903060042445763242)
XLA Ops:
  0.6 0.0 copy-start
  0.6 0.7 %copy-done = s32[8,2]{0,1:T(2,128)S(1)} copy-done((s32[8,2]{0,1:T(2,128)S(1)}, s32[8,2]{0,1:T(2,128)}, u32[]{:S(2)}) %copy-start) | copy-done | bytes 88
  1.3 62.7 %project.1 = (f32[32,1024]{1,0:T(8,128)S(1)}, f32[32,128]{1,0:T(8,128)S(1)}) custom-call(bf16[8,128,128]{2,1,0:T(8,128)(2,1)} %tiles.1, s32[2,8]{1,0:T(2,128)S(1)} %bitcast.1, bf16[128,1024]{1,0:T(8,128)(2,1)} %modes.1, bf16[1024,128]{1,0:T(8,128)(2,1)} %trial.1), custom_call_target="tpu_custom_call" | custom-call | tf_op jit(solution)/shard_map/project/pallas_call | solution.py:264
  64.0 0.7 %copy.8 = f32[32,1024]{1,0:T(8,128)} copy(f32[32,1024]{1,0:T(8,128)S(1)} %get-tuple-element.4) | data formatting | bytes 262144
  64.7 0.6 copy.9
Async XLA Ops:
  0.6 0.7 %copy-start = (s32[8,2]{0,1:T(2,128)S(1)}, s32[8,2]{0,1:T(2,128)}, u32[]{:S(2)}) copy-start(s32[8,2]{0,1:T(2,128)} %param.5) | copy-start | bytes 196
